TPU v7x, 32 devices: a whole 2x2x4 slice. The times are simulated.
32 devices in a mesh: parts: 2 (over y), latent: 16 (over z, x, core).
Axes of the slice: x: 2, y: 2, z: 4, core: 2. Of those that a mesh axis runs over, the one named last changes fastest.
Arguments:
- residual: bfloat16 [512, 4608], P(('parts', 'latent')), parts along dimension 0, may hold values from -6 to 6
- enc_weight: bfloat16 [4608, 8192], P(None, 'latent'), may hold values from -0.09375 to 0.09375
- enc_bias: float32 [8192], P('latent'), may hold values from -3 to 3
- threshold: float32 [8192], P('latent'), may hold values from 0.3 to 2
- dec_weight: bfloat16 [8192, 4608], P('latent'), may hold values from -0.1875 to 0.1875
- dec_bias: float32 [4608], replicated, may hold values from -3 to 3
- pre_gain: float32 [4608], replicated, may hold values from 0.1 to 1.9
- gate_weight: bfloat16 [4608, 2304], P(None, 'latent'), may hold values from -0.09375 to 0.09375
- up_weight: bfloat16 [4608, 2304], P(None, 'latent'), may hold values from -0.09375 to 0.09375
- down_weight: bfloat16 [2304, 4608], P('latent'), may hold values from -0.125 to 0.125
- post_gain: float32 [4608], replicated, may hold values from 0.1 to 1.9
Outputs:
- spliced_out: bfloat16 [512, 4608], P(('parts', 'latent')), parts along dimension 0
There are 2 independent parts, one for each index of `parts`. A program takes and returns all parts, laid end to end along the dimension named above; an argument that names none is the same for every part. Nothing has to cross between parts.
All inputs are finite; a program needn't handle non-finite values.
Results may differ from a plain program's by a relative error of at most 0.0057.
Values may be sent and summed in bfloat16 or wider, within the bound.
No kernel may reach another device: no remote copies, remote signals or barrier semaphores. Data moves between devices by JAX's collectives and lax.ppermute only.
A program may use at most 128 MiB of HBM per device.

v0:
```python
import jax
import jax.numpy as jnp
from jax import lax
from jax.sharding import PartitionSpec as P

sharpness = 10.0
epsilon = 1e-06


def rms_scale(values, gain):
    return values * lax.rsqrt(jnp.mean(values * values, axis=-1, keepdims=True) + epsilon) * gain


def per_device(
    residual,
    enc_weight,
    enc_bias,
    threshold,
    dec_weight,
    dec_bias,
    pre_gain,
    gate_weight,
    up_weight,
    down_weight,
    post_gain,
):

    def encode(block_rows):
        preact = jnp.dot(block_rows, enc_weight, preferred_element_type=jnp.float32) + enc_bias
        return (preact * jax.nn.sigmoid(sharpness * (preact - threshold))).astype(jnp.bfloat16)

    def feed_hidden(block_rows):
        gate_proj = jnp.dot(block_rows, gate_weight, preferred_element_type=jnp.float32)
        up_proj = jnp.dot(block_rows, up_weight, preferred_element_type=jnp.float32)
        return (jax.nn.gelu(gate_proj, approximate=True) * up_proj).astype(jnp.bfloat16)

    def splice(local_rows):
        latent_acts = encode(lax.all_gather(local_rows, "latent", axis=0, tiled=True))
        chosen = latent_acts
        rebuilt = (
            lax.psum_scatter(
                jnp.dot(chosen, dec_weight, preferred_element_type=jnp.float32),
                "latent",
                scatter_dimension=0,
                tiled=True,
            )
            + dec_bias
        )
        normed = rms_scale(rebuilt, pre_gain).astype(jnp.bfloat16)
        hidden = feed_hidden(lax.all_gather(normed, "latent", axis=0, tiled=True))
        chosen = hidden
        ffn_sum = lax.psum_scatter(
            jnp.dot(chosen, down_weight, preferred_element_type=jnp.float32),
            "latent",
            scatter_dimension=0,
            tiled=True,
        )
        return (rebuilt + rms_scale(ffn_sum, post_gain)).astype(jnp.bfloat16)

    portions = [residual]
    results = [splice(portion) for portion in portions]
    return results[0]


def solution(mesh):
    return jax.shard_map(
        per_device,
        mesh=mesh,
        in_specs=(
            P(("parts", "latent"), None),
            P(None, "latent"),
            P("latent"),
            P("latent"),
            P("latent", None),
            P(),
            P(),
            P(None, "latent"),
            P(None, "latent"),
            P("latent", None),
            P(),
        ),
        out_specs=P(("parts", "latent"), None),
        check_vma=False,
    )
```

profile of v0, /device:TPU:0, one launch (start us, length us, event | category | flops | bytes accessed | tf_op | source)
XLA Modules:
  0.0 276.6 jit_solution(1392521232975287917)
XLA Ops:
  6.5 0.0 copy-start
  6.5 0.0 all-gather.3.cloned.1.call-start
  6.5 0.7 all-gather.3.cloned.1.call-update
  7.3 0.0 reduce-scatter.3.cloned.1.call-start
  7.3 47.4 %all-gather.3.cloned.1.call-done = bf16[256,4608]{1,0:T(8,128)(2,1)} async-done(((bf16[16,4608]{1,0:T(8,128)(2,1)}), bf16[256,4608]{1,0:T(8,128)(2,1)}) %all-gather.3.cloned.1.call-update) | async-done | bytes 2359312 | tf_op jit(solution)/shard_map/all_gather | solution.py:38
  54.7 9.4 %fusion.2 = f32[256,4608]{1,0:T(8,128)} fusion(bf16[512,4608]{1,0:T(8,128)(2,1)} %param.15, bf16[256,4608]{1,0:T(8,128)(2,1)} %all-gather.3.cloned.1.call-done, bf16[4608,512]{1,0:T(8,128)(2,1)} %param.12, f32[512]{0:T(512)} %param.14, f32[512]{0:T(512)} %param.13), kind=kOutput, calls=%fused_computation.5 | convolution fusion | flops 2416967680 | bytes 16519168 | tf_op jit(solution)/shard_map/dot_general | solution.py:42
  64.1 0.0 reduce-scatter.3.cloned.1.call-update
  64.1 0.0 copy-start.2
  64.1 0.0 all-gather.5.cloned.1.call-start
  64.1 74.4 %reduce-scatter.3.cloned.1.call-done = f32[16,4608]{1,0:T(8,128)} async-done(((f32[256,4608]{1,0:T(8,128)}), f32[16,4608]{1,0:T(8,128)}) %reduce-scatter.3.cloned.1.call-update) | async-done | bytes 294928 | tf_op jit(solution)/shard_map/reduce_scatter | solution.py:41
  138.6 0.0 copy-done.3
  138.6 1.1 multiply_reduce_fusion.1
  139.7 0.0 copy-done.4
  139.7 1.7 multiply_convert_fusion.1
  141.4 0.0 all-gather.5.cloned.1.call-update
  141.4 0.0 reduce-scatter.5.cloned.1.call-start
  141.5 41.6 %all-gather.5.cloned.1.call-done = bf16[256,4608]{1,0:T(8,128)(2,1)} async-done(((bf16[16,4608]{1,0:T(8,128)(2,1)}), bf16[256,4608]{1,0:T(8,128)(2,1)}) %all-gather.5.cloned.1.call-update) | async-done | bytes 2359312 | tf_op jit(solution)/shard_map/all_gather | solution.py:50
  183.1 2.9 %fusion.25 = f32[256,144]{0,1:T(8,128)S(1)} fusion(bf16[256,4608]{1,0:T(8,128)(2,1)} %all-gather.5.cloned.1.call-done, bf16[4608,144]{0,1:T(8,128)(2,1)} %param.18), kind=kOutput, calls=%fused_computation.34 | convolution fusion | flops 339738624 | bytes 3833856 | tf_op jit(solution)/shard_map/dot_general | solution.py:33
  186.0 0.0 copy-done
  186.0 6.6 %fusion.1 = f32[256,4608]{1,0:T(8,128)} fusion(bf16[144,4608]{1,0:T(8,128)(2,1)S(1)} %copy-done, bf16[256,4608]{1,0:T(8,128)(2,1)} %all-gather.5.cloned.1.call-done, bf16[4608,144]{0,1:T(8,128)(2,1)S(1)} %copy-done.2, f32[256,144]{0,1:T(8,128)S(1)} %fusion.25), kind=kOutput, calls=%fused_computation.3 | convolution fusion | flops 679845888 | bytes 9879552 | tf_op jit(solution)/shard_map/dot_general | solution.py:53
  192.7 0.0 reduce-scatter.5.cloned.1.call-update
  192.7 74.5 %reduce-scatter.5.cloned.1.call-done = f32[16,4608]{1,0:T(8,128)} async-done(((f32[256,4608]{1,0:T(8,128)}), f32[16,4608]{1,0:T(8,128)}) %reduce-scatter.5.cloned.1.call-update) | async-done | bytes 294928 | tf_op jit(solution)/shard_map/reduce_scatter | solution.py:52
  267.2 1.1 multiply_reduce_fusion
  268.3 1.7 add_convert_fusion
  (9 shorter events, 0.0 us)
Async XLA Ops:
  6.5 179.5 %copy-start = (bf16[144,4608]{1,0:T(8,128)(2,1)S(1)}, bf16[144,4608]{1,0:T(8,128)(2,1)}, u32[]{:S(2)}) copy-start(bf16[144,4608]{1,0:T(8,128)(2,1)} %param.20) | copy-start | bytes 3981316
  6.5 48.1 %all-gather.3.cloned.1.call-start = ((), (), s32[]{:S(2)}) async-start(), calls=%async_computation.2 | async-start | bytes 2506752 | tf_op jit(solution)/shard_map/all_gather | solution.py:38
  7.3 131.3 %reduce-scatter.3.cloned.1.call-start = ((), (), s32[]{:S(2)}) async-start(), calls=%async_computation.3 | async-start | bytes 5013504 | tf_op jit(solution)/shard_map/reduce_scatter | solution.py:41
  64.1 74.5 %copy-start.3 = (f32[4608]{0:T(1024)S(1)}, f32[4608]{0:T(1024)}, u32[]{:S(2)}) copy-start(f32[4608]{0:T(1024)} %param.16) | copy-start | bytes 55300
  64.1 75.6 %copy-start.4 = (f32[4608]{0:T(1024)S(1)}, f32[4608]{0:T(1024)}, u32[]{:S(2)}) copy-start(f32[4608]{0:T(1024)} %param.17) | copy-start | bytes 55300
  64.1 122.0 %copy-start.2 = (bf16[4608,144]{0,1:T(8,128)(2,1)S(1)}, bf16[4608,144]{0,1:T(8,128)(2,1)}, u32[]{:S(2)}) copy-start(bf16[4608,144]{0,1:T(8,128)(2,1)} %param.19) | copy-start | bytes 3981316
  64.1 119.0 %all-gather.5.cloned.1.call-start = ((), (), s32[]{:S(2)}) async-start(), calls=%async_computation.4 | async-start | bytes 2506752 | tf_op jit(solution)/shard_map/all_gather | solution.py:50
  141.4 125.7 %reduce-scatter.5.cloned.1.call-start = ((), (), s32[]{:S(2)}) async-start(), calls=%async_computation.5 | async-start | bytes 5013504 | tf_op jit(solution)/shard_map/reduce_scatter | solution.py:52
  192.7 75.6 %copy-start.1 = (f32[16,4608]{1,0:T(8,128)S(1)}, f32[16,4608]{1,0:T(8,128)}, u32[]{:S(2)}) copy-start(f32[16,4608]{1,0:T(8,128)} %reduce-scatter.3.cloned.1.call-done) | copy-start | bytes 884740
  192.7 75.6 %copy-start.5 = (f32[4608]{0:T(1024)S(1)}, f32[4608]{0:T(1024)}, u32[]{:S(2)}) copy-start(f32[4608]{0:T(1024)} %param.21) | copy-start | bytes 55300
Sparse Core Ops, SparseCore 0:
  9.6 45.0 all-gather.2
  64.2 74.3 reduce-scatter.2
  141.5 41.4 all-gather.4
  192.8 74.3 reduce-scatter.4
where the time goes:
time: 277 us
  waiting for transfers between devices  239 us (86%)
  matrix products  18.9 us (7%)
  between operations  13.2 us (5%)
  other arithmetic  5.68 us (2%)
    reduce_scatter x1, waiting for transfers between devices, splice(): lax.psum_scatter(jnp.dot(chosen, down_weight, preferred_element_type=jnp....  74.5 us
    reduce_scatter x1, waiting for transfers between devices, splice(): lax.psum_scatter(jnp.dot(chosen, dec_weight, preferred_element_type=jnp.f...  74.4 us
    all_gather x1, waiting for transfers between devices, splice(): lax.all_gather(local_rows, 'latent', axis=0, tiled=True)  47.4 us
    all_gather x1, waiting for transfers between devices, splice(): hidden = feed_hidden(lax.all_gather(normed, 'latent', axis=0, tiled=True))  41.6 us
    dot_general x1, matrix products, splice(): jnp.dot(chosen, dec_weight, preferred_element_type=jnp.float32)  9.37 us
    dot_general x1, matrix products, splice(): jnp.dot(chosen, down_weight, preferred_element_type=jnp.float32)  6.61 us
  transfers between devices with their start and end apart: 4, of which 4 were waited for; matrix products, arithmetic and copies ran while one was open for 0% of the time, Pallas kernels for 0%

commit v1 on v0

--- a/solution.py
+++ b/solution.py
@@ -5,6 +5,22 @@
 
 sharpness = 10.0
 epsilon = 1e-06
+
+
+def group_the_leaves(body):
+    g_now = lax.psum(1, axis_name="latent")
+    built = lax.axis_index("latent")
+    f_now, left_arr = (g_now, built)
+    state_next, local_now = (body, 1)
+    while local_now < f_now:
+        back = lax.ppermute(
+            state_next, axis_name="latent", perm=[(d, d ^ local_now) for d in range(f_now)]
+        )
+        t1 = jnp.concatenate([state_next, back], 0)
+        current_arr = jnp.concatenate([back, state_next], 0)
+        state_next = jnp.where(left_arr & local_now == 0, t1, current_arr)
+        local_now = 2 * local_now
+    return state_next
 
 
 def rms_scale(values, gain):
@@ -35,7 +51,7 @@
         return (jax.nn.gelu(gate_proj, approximate=True) * up_proj).astype(jnp.bfloat16)
 
     def splice(local_rows):
-        latent_acts = encode(lax.all_gather(local_rows, "latent", axis=0, tiled=True))
+        latent_acts = encode(group_the_leaves(local_rows))
         chosen = latent_acts
         rebuilt = (
             lax.psum_scatter(

time: 277 us -> 313 us (1.13)
  waiting for transfers between devices: 239 us -> 265 us
  starting transfers between devices: 0.13 us -> 8.06 us
    ppermute x0 -> x4, waiting for transfers between devices: none -> 71.9 us  [group_the_leaves(): lax.ppermute(state_next, axis_name='latent', perm=[(d, d ^ local_now) for...]
    all_gather x1 -> x0, waiting for transfers between devices: 47.4 us -> none  [splice(): lax.all_gather(local_rows, 'latent', axis=0, tiled=True)]
    ppermute x0 -> x4, starting transfers between devices: none -> 7.98 us  [group_the_leaves(): lax.ppermute(state_next, axis_name='latent', perm=[(d, d ^ local_now) for...]
  transfers between devices with their start and end apart: 4 -> 7, of which waited for: 4 -> 7; matrix products, arithmetic and copies ran while one was open for 0% -> 0% of each run, Pallas kernels for 0% -> 0%
where the time goes in v1:
time: 313 us
  waiting for transfers between devices  265 us (85%)
  matrix products  18.8 us (6%)
  between operations  13.2 us (4%)
  other arithmetic  8.3 us (3%)
  starting transfers between devices  8.06 us (3%)
    reduce_scatter x1, waiting for transfers between devices, splice(): lax.psum_scatter(jnp.dot(chosen, dec_weight, preferred_element_type=jnp.f...  76.5 us
    reduce_scatter x1, waiting for transfers between devices, splice(): lax.psum_scatter(jnp.dot(chosen, down_weight, preferred_element_type=jnp....  74.4 us
    ppermute x4, waiting for transfers between devices, group_the_leaves(): lax.ppermute(state_next, axis_name='latent', perm=[(d, d ^ local_now) for...  71.9 us
    all_gather x1, waiting for transfers between devices, splice(): hidden = feed_hidden(lax.all_gather(normed, 'latent', axis=0, tiled=True))  41.6 us
    dot_general x1, matrix products, splice(): jnp.dot(chosen, dec_weight, preferred_element_type=jnp.float32)  9.3 us
    ppermute x4, starting transfers between devices, group_the_leaves(): lax.ppermute(state_next, axis_name='latent', perm=[(d, d ^ local_now) for...  7.98 us
    dot_general x1, matrix products, splice(): jnp.dot(chosen, down_weight, preferred_element_type=jnp.float32)  6.62 us
  transfers between devices with their start and end apart: 7, of which 7 were waited for; matrix products, arithmetic and copies ran while one was open for 0% of the time, Pallas kernels for 0%

profile of v1, /device:TPU:0, one launch (start us, length us, event | category | flops | bytes accessed | tf_op | source)
XLA Modules:
  0.0 312.9 jit_solution(793490148362850727)
XLA Ops:
  6.5 0.6 collective-permute-start
  7.1 1.2 collective-permute-done
  8.3 1.0 maximum_select_fusion.10
  9.4 2.9 collective-permute-start.1
  12.3 7.3 %collective-permute-done.1 = bf16[32,4608]{1,0:T(8,128)(2,1)S(1)} collective-permute-done((bf16[32,4608]{1,0:T(8,128)(2,1)S(1)}, bf16[32,4608]{1,0:T(8,128)(2,1)S(1)}, u32[]{:S(2)}, u32[]{:S(2)}) %collective-permute-start.1) | collective-permute-done | bytes 294944 | tf_op jit(solution)/shard_map/ppermute | solution.py:16
  19.6 0.1 maximum_select_fusion.5
  19.7 1.9 collective-permute-start.2
  21.6 13.1 %collective-permute-done.2 = bf16[64,4608]{1,0:T(8,128)(2,1)} collective-permute-done((bf16[64,4608]{1,0:T(8,128)(2,1)S(1)}, bf16[64,4608]{1,0:T(8,128)(2,1)}, u32[]{:S(2)}, u32[]{:S(2)}) %collective-permute-start.2) | collective-permute-done | bytes 589856 | tf_op jit(solution)/shard_map/ppermute | solution.py:16
  34.7 1.5 maximum_select_fusion.4
  36.1 2.6 collective-permute-start.3
  38.8 50.3 %collective-permute-done.3 = bf16[128,4608]{1,0:T(8,128)(2,1)} collective-permute-done((bf16[128,4608]{1,0:T(8,128)(2,1)S(1)}, bf16[128,4608]{1,0:T(8,128)(2,1)}, u32[]{:S(2)}, u32[]{:S(2)}) %collective-permute-start.3) | collective-permute-done | bytes 1179680 | tf_op jit(solution)/shard_map/ppermute | solution.py:16
  89.1 9.3 %fusion.10 = f32[256,4608]{1,0:T(8,128)} fusion(bf16[512,4608]{1,0:T(8,128)(2,1)} %param.15, bf16[4608,512]{1,0:T(8,128)(2,1)} %param.12, bf16[128,4608]{1,0:T(8,128)(2,1)} %collective-permute-done.3, bf16[128,4608]{1,0:T(8,128)(2,1)S(1)} %maximum_select_fusion.4, pred[]{:T(512)S(6)} %eq.12, f32[512]{0:T(512)S(1)} %copy-done.6, f32[512]{0:T(512)S(1)} %copy-done.7), kind=kOutput, calls=%fused_computation.15 | convolution fusion | flops 2427584512 | bytes 16519169 | tf_op jit(solution)/shard_map/dot_general | solution.py:58
  98.4 0.0 reduce-scatter.3.cloned.1.call-update
  98.4 0.0 all-gather.2.cloned.1.call-start
  98.5 76.5 %reduce-scatter.3.cloned.1.call-done = f32[16,4608]{1,0:T(8,128)} async-done(((f32[256,4608]{1,0:T(8,128)}), f32[16,4608]{1,0:T(8,128)}) %reduce-scatter.3.cloned.1.call-update) | async-done | bytes 294928 | tf_op jit(solution)/shard_map/reduce_scatter | solution.py:57
  175.0 1.1 multiply_reduce_fusion.1
  176.1 1.7 multiply_convert_fusion.1
  177.9 0.0 reduce-scatter.5.cloned.1.call-start
  177.9 41.6 %all-gather.2.cloned.1.call-done = bf16[256,4608]{1,0:T(8,128)(2,1)} async-done(((bf16[16,4608]{1,0:T(8,128)(2,1)}), bf16[256,4608]{1,0:T(8,128)(2,1)}) %all-gather.2.cloned.1.call-update) | async-done | bytes 2359312 | tf_op jit(solution)/shard_map/all_gather | solution.py:66
  219.5 2.9 fusion.35
  222.5 6.6 %fusion.9 = f32[256,4608]{1,0:T(8,128)} fusion(bf16[144,4608]{1,0:T(8,128)(2,1)S(1)} %copy-done, bf16[256,4608]{1,0:T(8,128)(2,1)} %all-gather.2.cloned.1.call-done, bf16[4608,144]{0,1:T(8,128)(2,1)S(1)} %copy-done.2, f32[256,144]{0,1:T(8,128)S(1)} %fusion.35), kind=kOutput, calls=%fused_computation.12 | convolution fusion | flops 679845888 | bytes 9879552 | tf_op jit(solution)/shard_map/dot_general | solution.py:69
  229.1 74.4 %reduce-scatter.5.cloned.1.call-done = f32[16,4608]{1,0:T(8,128)} async-done(((f32[256,4608]{1,0:T(8,128)}), f32[16,4608]{1,0:T(8,128)}) %reduce-scatter.5.cloned.1.call-update) | async-done | bytes 294928 | tf_op jit(solution)/shard_map/reduce_scatter | solution.py:68
  303.5 1.1 multiply_reduce_fusion
  304.7 1.7 add_convert_fusion
  (21 shorter events, 0.1 us)
Async XLA Ops:
  6.5 215.9 %copy-start = (bf16[144,4608]{1,0:T(8,128)(2,1)S(1)}, bf16[144,4608]{1,0:T(8,128)(2,1)}, u32[]{:S(2)}) copy-start(bf16[144,4608]{1,0:T(8,128)(2,1)} %param.20) | copy-start | bytes 3981316
  6.5 82.5 %copy-start.6 = (f32[512]{0:T(512)S(1)}, f32[512]{0:T(512)}, u32[]{:S(2)}) copy-start(f32[512]{0:T(512)} %param.14) | copy-start | bytes 6148
  6.5 82.5 %copy-start.7 = (f32[512]{0:T(512)S(1)}, f32[512]{0:T(512)}, u32[]{:S(2)}) copy-start(f32[512]{0:T(512)} %param.13) | copy-start | bytes 6148
  6.5 168.4 %reduce-scatter.3.cloned.1.call-start = ((), (), s32[]{:S(2)}) async-start(), calls=%async_computation.2 | async-start | bytes 5013504 | tf_op jit(solution)/shard_map/reduce_scatter | solution.py:57
  6.5 1.8 collective-permute-start
  9.4 10.2 %collective-permute-start.1 = (bf16[32,4608]{1,0:T(8,128)(2,1)S(1)}, bf16[32,4608]{1,0:T(8,128)(2,1)S(1)}, u32[]{:S(2)}, u32[]{:S(2)}) collective-permute-start(bf16[32,4608]{1,0:T(8,128)(2,1)S(1)} %maximum_select_fusion.10), channel_id=1, source_target_pairs={{0,2},{1,3},{2,0},{3,1},{4,6},{5,7},{6,4},{7,5},{8,10},{9,11},{10,... | collective-permute-start | bytes 884744 | tf_op jit(solution)/shard_map/ppermute | solution.py:16
  19.7 15.0 %collective-permute-start.2 = (bf16[64,4608]{1,0:T(8,128)(2,1)S(1)}, bf16[64,4608]{1,0:T(8,128)(2,1)}, u32[]{:S(2)}, u32[]{:S(2)}) collective-permute-start(bf16[64,4608]{1,0:T(8,128)(2,1)S(1)} %maximum_select_fusion.5), channel_id=1, source_target_pairs={{0,4},{1,5},{2,6},{3,7},{4,0},{5,1},{6,2},{7,3},{8,12},{9,13},{10,... | collective-permute-start | bytes 1769480 | tf_op jit(solution)/shard_map/ppermute | solution.py:16
  36.1 52.9 %collective-permute-start.3 = (bf16[128,4608]{1,0:T(8,128)(2,1)S(1)}, bf16[128,4608]{1,0:T(8,128)(2,1)}, u32[]{:S(2)}, u32[]{:S(2)}) collective-permute-start(bf16[128,4608]{1,0:T(8,128)(2,1)S(1)} %maximum_select_fusion.4), channel_id=1, source_target_pairs={{0,8},{1,9},{2,10},{3,11},{4,12},{5,13},{6,14},{7,15},{8,0},{9,1},... | collective-permute-start | bytes 3538952 | tf_op jit(solution)/shard_map/ppermute | solution.py:16
  98.4 76.6 %copy-start.3 = (f32[4608]{0:T(1024)S(1)}, f32[4608]{0:T(1024)}, u32[]{:S(2)}) copy-start(f32[4608]{0:T(1024)} %param.16) | copy-start | bytes 55300
  98.4 77.7 %copy-start.4 = (f32[4608]{0:T(1024)S(1)}, f32[4608]{0:T(1024)}, u32[]{:S(2)}) copy-start(f32[4608]{0:T(1024)} %param.17) | copy-start | bytes 55300
  98.4 124.0 %copy-start.2 = (bf16[4608,144]{0,1:T(8,128)(2,1)S(1)}, bf16[4608,144]{0,1:T(8,128)(2,1)}, u32[]{:S(2)}) copy-start(bf16[4608,144]{0,1:T(8,128)(2,1)} %param.19) | copy-start | bytes 3981316
  98.4 121.1 %all-gather.2.cloned.1.call-start = ((), (), s32[]{:S(2)}) async-start(), calls=%async_computation.3 | async-start | bytes 2506752 | tf_op jit(solution)/shard_map/all_gather | solution.py:66
  177.9 125.7 %reduce-scatter.5.cloned.1.call-start = ((), (), s32[]{:S(2)}) async-start(), calls=%async_computation.4 | async-start | bytes 5013504 | tf_op jit(solution)/shard_map/reduce_scatter | solution.py:68
  229.1 75.6 %copy-start.1 = (f32[16,4608]{1,0:T(8,128)S(1)}, f32[16,4608]{1,0:T(8,128)}, u32[]{:S(2)}) copy-start(f32[16,4608]{1,0:T(8,128)} %reduce-scatter.3.cloned.1.call-done) | copy-start | bytes 884740
  229.1 75.6 %copy-start.5 = (f32[4608]{0:T(1024)S(1)}, f32[4608]{0:T(1024)}, u32[]{:S(2)}) copy-start(f32[4608]{0:T(1024)} %param.21) | copy-start | bytes 55300
Sparse Core Ops, SparseCore 0:
  98.5 76.4 reduce-scatter.2
  178.0 41.4 all-gather.1
  229.2 74.2 reduce-scatter.4
